TPU v7x, 256 devices: a whole 4x4x8 slice. The times are simulated.
256 devices in a mesh: gx: 8 (over x_hi, y), gy: 16 (over z, x_lo), af: 2 (over core).
Axes of the slice: x: 4 (x_hi: 2, x_lo: 2; x = x_hi * 2 + x_lo), y: 4, z: 8, core: 2. Of those that a mesh axis runs over, the one named last changes fastest.
Arguments:
- model: float32 [256, 512, 128], P('gx', 'gy'), may hold values from 0.5 to 2
- freq_sq: float32 [4], P('af'), may hold values from 0.5 to 3
- source: float32 [4, 2, 256, 512, 128], P('af', None, 'gx', 'gy'), may hold values from -20 to 20
- observed: float32 [4, 2, 256, 512], P('af', None, 'gx', 'gy'), may hold values from -6 to 6
- receiver_depth: int32 [256, 512], P('gx', 'gy'), may hold values from 0 to 3
Outputs:
- wavefield: float32 [4, 2, 256, 512, 128], P('af', None, 'gx', 'gy')
- gradient: float32 [256, 512, 128], P('gx', 'gy')
Inputs may be any that keep to these rules, and one draw needn't show every extreme that they name: `receiver_depth`: every surface column holds one receiver, at the given depth index.
All inputs are finite; a program needn't handle non-finite values.
Results may differ from a plain program's by a relative error of at most 0.00012.
Values sent between devices are 32-bit elements; how exact they have to be, the bound alone decides.
A program may use at most 64 MiB of HBM per device.

v0:
```python
import jax
import jax.numpy as jnp
from jax import lax
from jax.sharding import PartitionSpec as P

ITERS = 2
attenuation = 0.2
penalty = 4.0


def padded_2(cells, sides, width):
    for axis, dim in sides:
        count = lax.axis_size(axis)
        ends = count - 1
        head = lax.slice_in_dim(cells, 0, width, axis=dim)
        tail = lax.slice_in_dim(cells, cells.shape[dim] - width, cells.shape[dim], axis=dim)
        cells = jnp.concatenate(
            [
                lax.ppermute(tail, axis, [(i, (i + 1) % count) for i in range(ends)]),
                cells,
                lax.ppermute(head, axis, [((i + 1) % count, i) for i in range(ends)]),
            ],
            axis=dim,
        )
    return cells


def stencil_sum(padded):
    center = padded[:, :, 1:-1, 1:-1]
    total = padded[:, :, 2:, 1:-1] + padded[:, :, :-2, 1:-1]
    total = total + padded[:, :, 1:-1, 2:] + padded[:, :, 1:-1, :-2]
    upper = jnp.pad(center[..., 1:], ((0, 0), (0, 0), (0, 0), (0, 0), (0, 1)))
    lower = jnp.pad(center[..., :-1], ((0, 0), (0, 0), (0, 0), (0, 0), (1, 0)))
    return (center, total + upper + lower)


def apply_coef(coef_real, coef_imag, field, sign):
    real_part = coef_real * field[:, 0] - sign * coef_imag * field[:, 1]
    imag_part = coef_real * field[:, 1] + sign * coef_imag * field[:, 0]
    return jnp.stack([real_part, imag_part], axis=1)


def beside(field):
    padded = padded_2(field, (("gx", 2), ("gy", 3)), 1)
    center, total = stencil_sum(padded)
    return total


def inner(left, right):
    return jnp.sum(left * right, axis=(1, 2, 3, 4))


def expand(values):
    return values[:, None, None, None, None]


def on_device(model, freq_sq, source, observed, receiver_depth):
    squared = freq_sq[:, None, None, None]
    coef_real = 6.0 - squared * model[None]
    coef_imag = attenuation * squared * model[None]
    levels = lax.broadcasted_iota(jnp.int32, model.shape, 2)
    onehot = (levels == receiver_depth[:, :, None]).astype(jnp.float32)
    weights = penalty * onehot

    def forward(field):
        return apply_coef(coef_real, coef_imag, field, 1.0) - beside(field)

    def adjoint(field):
        return apply_coef(coef_real, coef_imag, field, -1.0) - beside(field)

    rhs = adjoint(source) + weights * observed[:, :, :, :, None]
    field = jnp.zeros_like(rhs)
    resid = rhs

    def squares(values):
        return lax.psum(inner(values, values), ("gx", "gy"))

    direction = rhs
    norm_now = squares(resid)
    for sweep in range(ITERS):
        image = adjoint(forward(direction)) + weights * direction
        alpha = norm_now / lax.psum(inner(direction, image), ("gx", "gy"))
        field = field + expand(alpha) * direction
        resid = resid - expand(alpha) * image
        norm_next = squares(resid)
        direction = resid + expand(norm_next / norm_now) * direction
        norm_now = norm_next
    misfit = forward(field) - source
    deriv_real = -squared
    deriv_imag = attenuation * squared
    wave_real = deriv_real * field[:, 0] - deriv_imag * field[:, 1]
    wave_imag = deriv_real * field[:, 1] + deriv_imag * field[:, 0]
    local_terms = jnp.sum(wave_real * misfit[:, 0] + wave_imag * misfit[:, 1], axis=0)
    gradient = lax.psum(local_terms, "af")
    return (field, gradient)


def solution(mesh):
    in_specs = (
        P("gx", "gy", None),
        P("af"),
        P("af", None, "gx", "gy", None),
        P("af", None, "gx", "gy"),
        P("gx", "gy"),
    )
    out_specs = (P("af", None, "gx", "gy", None), P("gx", "gy", None))
    return jax.shard_map(
        on_device, mesh=mesh, in_specs=in_specs, out_specs=out_specs, check_vma=False
    )
```

profile of v0, /device:TPU:1, one launch (start us, length us, event | category | flops | bytes accessed | tf_op | source)
XLA Modules:
  0.0 1227.7 jit_solution(6360724979951832859)
XLA Ops:
  9.6 4.8 collective-permute-start.1
  14.4 2.8 copy.48
  17.5 2.8 fusion.79
  24.2 4.0 collective-permute-start.3
  30.8 7.4 fusion.45
  39.6 4.0 collective-permute-start.5
  46.2 4.3 collective-permute-start.7
  55.6 4.6 collective-permute-start.9
  62.8 4.9 collective-permute-start.11
  69.3 4.1 multiply_reduce_fusion.1
  73.4 305.5 %all-reduce.12 = (f32[2]{0:T(128)S(1)}, f32[2]{0:T(128)S(1)}) all-reduce(f32[2]{0:T(128)S(1)} %get-tuple-element.7, f32[2]{0:T(128)S(1)} %get-tuple-element.6), channel_id=1, replica_groups=mesh['gx'=8,'gy'=16,'af'=2] {'gx','gy'}, use_global_device_ids=true, to_apply=%region_1.2 | all-reduce | flops 4 | bytes 32 | tf_op jit(solution)/shard_map/psum | solution.py:76
  381.0 286.8 %psum.37 = f32[2]{0:T(128)S(1)} all-reduce(f32[2]{0:T(128)S(1)} %multiply_reduce_fusion), channel_id=1, replica_groups=mesh['gx'=8,'gy'=16,'af'=2] {'gx','gy'}, use_global_device_ids=true, to_apply=%region_5.6 | all-reduce | flops 2 | bytes 16 | tf_op jit(solution)/shard_map/psum | solution.py:76
  667.8 2.2 multiply_add_fusion.1
  671.4 4.2 collective-permute-start.13
  678.0 4.1 collective-permute-start.15
  687.0 4.3 collective-permute-start.17
  694.0 4.9 collective-permute-start.19
  700.8 3.0 fusion.19
  703.8 289.7 %psum.38 = f32[2]{0:T(128)S(1)} all-reduce(f32[2]{0:T(128)S(1)} %fusion.19), channel_id=1, replica_groups=mesh['gx'=8,'gy'=16,'af'=2] {'gx','gy'}, use_global_device_ids=true, to_apply=%region_7.8 | all-reduce | flops 2 | bytes 16 | tf_op jit(solution)/shard_map/psum | solution.py:82
  998.3 4.0 collective-permute-start.21
  1005.0 4.1 collective-permute-start.23
  1010.6 2.7 fusion.10
  1014.7 4.1 copy.70
  1018.8 199.9 %all-reduce.15.cloned.1.call-done = f32[32,32,128]{2,0,1:T(8,128)} async-done(((f32[32,32,128]{2,0,1:T(8,128)}), f32[32,32,128]{2,0,1:T(8,128)}) %all-reduce.15.cloned.1.call-update) | async-done | bytes 524304 | tf_op jit(solution)/shard_map/psum | solution.py:94
  (93 shorter events, 49.9 us)
Async XLA Ops:
  7.2 1211.5 %all-reduce.15.cloned.1.call-start = ((), (), s32[]{:S(2)}) async-start(), calls=%async_computation | async-start | bytes 1048576 | tf_op jit(solution)/shard_map/psum | solution.py:94
  8.2 14.1 %collective-permute-start = (f32[2,2,1,32,128]{4,2,3,0,1:T(1,128)S(1)}, f32[2,2,1,32,128]{4,2,3,0,1:T(1,128)S(1)}, u32[]{:S(2)}, u32[]{:S(2)}) collective-permute-start(f32[2,2,1,32,128]{4,2,3,0,1:T(1,128)S(1)} %copy.50), channel_id=1, source_target_pairs={{32,0},{64,32},{96,64},{128,96},{160,128},{192,160},{224,192},{33,... | collective-permute-start | bytes 196616 | tf_op jit(solution)/shard_map/ppermute | solution.py:21
  9.6 12.7 %collective-permute-start.1 = (f32[2,2,1,32,128]{4,2,3,0,1:T(1,128)S(1)}, f32[2,2,1,32,128]{4,2,3,0,1:T(1,128)S(1)}, u32[]{:S(2)}, u32[]{:S(2)}) collective-permute-start(f32[2,2,1,32,128]{4,2,3,0,1:T(1,128)S(1)} %copy.52), channel_id=1, source_target_pairs={{0,32},{32,64},{64,96},{96,128},{128,160},{160,192},{192,224},{1,3... | collective-permute-start | bytes 196616 | tf_op jit(solution)/shard_map/ppermute | solution.py:19
  22.9 6.4 collective-permute-start.2
  24.2 6.6 collective-permute-start.3
  38.3 6.1 collective-permute-start.4
  39.6 5.3 collective-permute-start.5
  44.9 6.0 collective-permute-start.6
  46.2 5.8 collective-permute-start.7
  54.3 6.7 collective-permute-start.8
  55.6 5.9 collective-permute-start.9
  61.5 6.6 collective-permute-start.10
  62.8 6.5 collective-permute-start.11
  670.1 6.2 collective-permute-start.12
  671.4 5.3 collective-permute-start.13
  676.7 5.8 collective-permute-start.14
  678.0 5.6 collective-permute-start.15
  685.7 6.4 collective-permute-start.16
  687.0 5.6 collective-permute-start.17
  692.7 6.6 collective-permute-start.18
  694.0 6.8 collective-permute-start.19
  997.0 5.5 collective-permute-start.20
  1003.6 5.8 collective-permute-start.22
  1005.0 5.6 collective-permute-start.23
  (8 other events, 81.4 us)
Sparse Core Ops, SparseCore 0:
  1014.8 203.8 all-reduce.14
where the time goes:
time: 1230 us
  blocking collectives  882 us (72%)
  waiting for transfers between devices  210 us (17%)
  starting transfers between devices  67.7 us (6%)
  other arithmetic  34.7 us (3%)
  local copies, waits for them, and re-layouts  18.4 us (1%)
  between operations  14.6 us (1%)
    psum x2, blocking collectives, squares(): return lax.psum(inner(values, values), ('gx', 'gy'))  592 us
    psum x1, blocking collectives, on_device(): alpha = norm_now / lax.psum(inner(direction, image), ('gx', 'gy'))  290 us
    psum x1, waiting for transfers between devices, on_device(): gradient = lax.psum(local_terms, 'af')  200 us
    ppermute x12, starting transfers between devices, padded_2(): lax.ppermute(tail, axis, [(i, (i + 1) % count) for i in range(ends)])  52.2 us
  transfers between devices with their start and end apart: 25, of which 12 were waited for; matrix products, arithmetic and copies ran while one was open for 1% of the time, Pallas kernels for 0%

commit v1 on v0

--- a/solution.py
+++ b/solution.py
@@ -2,10 +2,12 @@
 import jax.numpy as jnp
 from jax import lax
 from jax.sharding import PartitionSpec as P
+from jax.lax import psum
 
 ITERS = 2
 attenuation = 0.2
 penalty = 4.0
+_manage_axis_part = lambda array_here: psum(psum(array_here, axis_name="gx"), axis_name="gy")
 
 
 def padded_2(cells, sides, width):
@@ -79,7 +81,7 @@
     norm_now = squares(resid)
     for sweep in range(ITERS):
         image = adjoint(forward(direction)) + weights * direction
-        alpha = norm_now / lax.psum(inner(direction, image), ("gx", "gy"))
+        alpha = norm_now / _manage_axis_part(inner(direction, image))
         field = field + expand(alpha) * direction
         resid = resid - expand(alpha) * image
         norm_next = squares(resid)

time: 1230 us -> 1000 us (0.81)
  blocking collectives: 882 us -> 681 us
  waiting for transfers between devices: 210 us -> 185 us
    psum x1 -> x4, blocking collectives: 290 us -> 104 us  [the longest x2 59.3 us: psum(psum(array_here, axis_name='gx'), axis_name='gy')]
    psum x1, waiting for transfers between devices: 200 us -> 175 us  [on_device(): gradient = lax.psum(local_terms, 'af')]
    psum x2, blocking collectives: 592 us -> 577 us  [squares(): return lax.psum(inner(values, values), ('gx', 'gy'))]
  transfers between devices with their start and end apart: 25 -> 25, of which waited for: 12 -> 12; matrix products, arithmetic and copies ran while one was open for 1% -> 2% of each run, Pallas kernels for 0% -> 0%
where the time goes in v1:
time: 1000 us
  blocking collectives  681 us (68%)
  waiting for transfers between devices  185 us (18%)
  starting transfers between devices  68.1 us (7%)
  other arithmetic  34.6 us (3%)
  local copies, waits for them, and re-layouts  18.4 us (2%)
  between operations  14.6 us (1%)
    psum x2, blocking collectives, squares(): return lax.psum(inner(values, values), ('gx', 'gy'))  577 us
    psum x1, waiting for transfers between devices, on_device(): gradient = lax.psum(local_terms, 'af')  175 us
    psum x2, blocking collectives, psum(psum(array_here, axis_name='gx'), axis_name='gy')  59.3 us
    ppermute x12, starting transfers between devices, padded_2(): lax.ppermute(tail, axis, [(i, (i + 1) % count) for i in range(ends)])  52.6 us
    psum x2, blocking collectives, psum(array_here, axis_name='gx')  44.3 us
  transfers between devices with their start and end apart: 25, of which 12 were waited for; matrix products, arithmetic and copies ran while one was open for 2% of the time, Pallas kernels for 0%

profile of v1, /device:TPU:1, one launch (start us, length us, event | category | flops | bytes accessed | tf_op | source)
XLA Modules:
  0.0 1002.1 jit_solution(7153647552932762608)
XLA Ops:
  9.6 4.8 collective-permute-start.1
  14.4 2.8 copy.48
  24.1 4.0 collective-permute-start.3
  30.7 7.4 fusion.45
  39.5 4.0 collective-permute-start.5
  46.1 4.3 collective-permute-start.7
  55.5 4.6 collective-permute-start.9
  62.7 4.9 collective-permute-start.11
  69.2 4.1 multiply_reduce_fusion.1
  73.3 27.1 %psum.50 = f32[2]{0:T(128)S(1)} all-reduce(f32[2]{0:T(128)S(1)} %get-tuple-element.6), channel_id=1, replica_groups=mesh['gx'=8,'gy'=16,'af'=2] {'gx'}, use_global_device_ids=true, to_apply=%region_3.4 | all-reduce | flops 2 | bytes 16 | tf_op jit(solution)/shard_map/psum | solution.py:10
  100.3 32.5 %psum.51 = f32[2]{0:T(128)S(1)} all-reduce(f32[2]{0:T(128)S(1)} %psum.50), channel_id=1, replica_groups=mesh['gx'=8,'gy'=16,'af'=2] {'gy'}, use_global_device_ids=true, to_apply=%region_4.5 | all-reduce | flops 2 | bytes 16 | tf_op jit(solution)/shard_map/psum | solution.py:10
  132.8 290.5 %psum.49 = f32[2]{0:T(128)S(1)} all-reduce(f32[2]{0:T(128)S(1)} %get-tuple-element.7), channel_id=1, replica_groups=mesh['gx'=8,'gy'=16,'af'=2] {'gx','gy'}, use_global_device_ids=true, to_apply=%region_1.2 | all-reduce | flops 2 | bytes 16 | tf_op jit(solution)/shard_map/psum | solution.py:78
  425.4 287.0 %psum.52 = f32[2]{0:T(128)S(1)} all-reduce(f32[2]{0:T(128)S(1)} %multiply_reduce_fusion), channel_id=1, replica_groups=mesh['gx'=8,'gy'=16,'af'=2] {'gx','gy'}, use_global_device_ids=true, to_apply=%region_6.7 | all-reduce | flops 2 | bytes 16 | tf_op jit(solution)/shard_map/psum | solution.py:78
  716.0 4.2 collective-permute-start.13
  722.6 4.2 collective-permute-start.15
  731.7 4.6 collective-permute-start.17
  739.0 4.9 collective-permute-start.19
  745.8 3.0 fusion.19
  748.8 17.2 %psum.53 = f32[2]{0:T(128)S(1)} all-reduce(f32[2]{0:T(128)S(1)} %fusion.19), channel_id=1, replica_groups=mesh['gx'=8,'gy'=16,'af'=2] {'gx'}, use_global_device_ids=true, to_apply=%region_8.9 | all-reduce | flops 2 | bytes 16 | tf_op jit(solution)/shard_map/psum | solution.py:10
  766.0 26.8 %psum.54 = f32[2]{0:T(128)S(1)} all-reduce(f32[2]{0:T(128)S(1)} %psum.53), channel_id=1, replica_groups=mesh['gx'=8,'gy'=16,'af'=2] {'gy'}, use_global_device_ids=true, to_apply=%region_9.10 | all-reduce | flops 2 | bytes 16 | tf_op jit(solution)/shard_map/psum | solution.py:10
  797.6 4.0 collective-permute-start.21
  804.2 4.1 collective-permute-start.23
  814.0 4.1 copy.70
  818.1 175.1 %all-reduce.14.cloned.1.call-done = f32[32,32,128]{2,0,1:T(8,128)} async-done(((f32[32,32,128]{2,0,1:T(8,128)}), f32[32,32,128]{2,0,1:T(8,128)}) %all-reduce.14.cloned.1.call-update) | async-done | bytes 524304 | tf_op jit(solution)/shard_map/psum | solution.py:96
  (96 shorter events, 57.5 us)
Async XLA Ops:
  7.2 986.0 %all-reduce.14.cloned.1.call-start = ((), (), s32[]{:S(2)}) async-start(), calls=%async_computation | async-start | bytes 1048576 | tf_op jit(solution)/shard_map/psum | solution.py:96
  8.2 14.0 %collective-permute-start = (f32[2,2,1,32,128]{4,2,3,0,1:T(1,128)S(1)}, f32[2,2,1,32,128]{4,2,3,0,1:T(1,128)S(1)}, u32[]{:S(2)}, u32[]{:S(2)}) collective-permute-start(f32[2,2,1,32,128]{4,2,3,0,1:T(1,128)S(1)} %copy.50), channel_id=1, source_target_pairs={{32,0},{64,32},{96,64},{128,96},{160,128},{192,160},{224,192},{33,... | collective-permute-start | bytes 196616 | tf_op jit(solution)/shard_map/ppermute | solution.py:23
  9.6 12.6 %collective-permute-start.1 = (f32[2,2,1,32,128]{4,2,3,0,1:T(1,128)S(1)}, f32[2,2,1,32,128]{4,2,3,0,1:T(1,128)S(1)}, u32[]{:S(2)}, u32[]{:S(2)}) collective-permute-start(f32[2,2,1,32,128]{4,2,3,0,1:T(1,128)S(1)} %copy.52), channel_id=1, source_target_pairs={{0,32},{32,64},{64,96},{96,128},{128,160},{160,192},{192,224},{1,3... | collective-permute-start | bytes 196616 | tf_op jit(solution)/shard_map/ppermute | solution.py:21
  22.9 6.4 collective-permute-start.2
  24.1 6.6 collective-permute-start.3
  38.2 6.1 collective-permute-start.4
  39.5 5.3 collective-permute-start.5
  44.8 6.0 collective-permute-start.6
  46.1 5.8 collective-permute-start.7
  54.2 6.7 collective-permute-start.8
  55.5 5.9 collective-permute-start.9
  61.4 6.6 collective-permute-start.10
  62.7 6.5 collective-permute-start.11
  714.7 6.2 collective-permute-start.12
  716.0 5.3 collective-permute-start.13
  721.3 5.9 collective-permute-start.14
  722.6 5.7 collective-permute-start.15
  730.4 6.7 collective-permute-start.16
  731.7 5.9 collective-permute-start.17
  737.7 6.6 collective-permute-start.18
  739.0 6.8 collective-permute-start.19
  796.3 5.5 collective-permute-start.20
  802.9 5.8 collective-permute-start.22
  804.2 5.6 collective-permute-start.23
  (8 other events, 81.7 us)
Sparse Core Ops, SparseCore 0:
  814.1 179.0 all-reduce.13
